TPU v7x, 32 devices: a whole 2x2x4 slice. The times are simulated.
32 devices in a mesh: ctx: 8 (over z, y), grp: 4 (over x, core).
Axes of the slice: x: 2, y: 2, z: 4, core: 2. Of those that a mesh axis runs over, the one named last changes fastest.
Arguments:
- streams: bfloat16 [3, 3072, 4096], P(None, 'ctx', 'grp'), may hold values from -400 to 400
- filters: bfloat16 [3, 256, 128], P(None, 'grp'), may hold values from -0.5 to 0.5
- gain: float32 [4096], P('grp'), may hold values from 0.5 to 1.5
Outputs:
- normed: bfloat16 [3072, 4096], P('ctx', 'grp')
All inputs are finite; a program needn't handle non-finite values.
Results may differ from a plain program's by a relative error of at most 0.012.
The roundings to bfloat16 on the way count: a program that leaves them out, or rounds other values in their place, can miss the bound.
Values may be sent and summed in bfloat16 or wider, within the bound.
A program may use at most 128 MiB of HBM per device.

v0:
```python
import math
import jax
import jax.numpy as jnp
import numpy as np
from jax import lax
from jax.sharding import PartitionSpec as P

HD = 128
CH = 4096


def passed_along(block, axis, distance):
    devices = range(lax.axis_size(axis))
    route = [(i - distance, i) for i in devices if i - distance in devices]
    return lax.ppermute(block, axis, route)


def filter_all(streams, filters):
    tok_rows = streams.shape[1]
    chan_count = streams.shape[2]
    filt_len = filters.shape[2]
    group_count = filters.shape[1]
    group_width = chan_count // group_count
    tail = streams[:, tok_rows - filt_len :, :]
    before = passed_along(tail, "ctx", 1)
    padded = jnp.concatenate([before, streams], axis=1)
    block_count = tok_rows // filt_len
    blocks = padded.reshape(3, block_count + 1, filt_len, group_count, group_width)
    lag_table = np.arange(filt_len)[:, None] - np.arange(filt_len)[None, :]
    lower_idx = np.where(lag_table >= 0, lag_table, 0)
    upper_idx = np.where(lag_table < 0, lag_table + filt_len, 0)
    lower = jnp.where(lag_table >= 0, filters[:, :, lower_idx], 0.0)
    upper = jnp.where(lag_table < 0, filters[:, :, upper_idx], 0.0)
    result = jnp.einsum(
        "agts,absgc->abtgc", lower, blocks[:, 1:], preferred_element_type=jnp.float32
    )
    result = result + jnp.einsum(
        "agts,absgc->abtgc", upper, blocks[:, :-1], preferred_element_type=jnp.float32
    )
    return result.reshape(3, tok_rows, chan_count).astype(jnp.bfloat16)


def attend(queries, positions, keyed, valued):
    tok_rows, chan_count = queries.shape
    head_count = chan_count // HD
    scale = HD ** (-0.5)
    query_heads = queries.reshape(tok_rows, head_count, HD)
    query_last = jnp.max(positions)
    start_state = (
        jnp.full((head_count, tok_rows), -1e30, jnp.float32),
        jnp.zeros((head_count, tok_rows), jnp.float32),
        jnp.zeros((tok_rows, head_count, HD), jnp.float32),
    )
    key_piece = lax.all_gather(keyed, "ctx", axis=0, tiled=True)
    value_piece = lax.all_gather(valued, "ctx", axis=0, tiled=True)
    piece_len = key_piece.shape[0]
    block_len = math.gcd(piece_len, 512)

    def step_block(step_idx, state):
        offset = step_idx * block_len
        key_block = lax.dynamic_slice_in_dim(key_piece, offset, block_len, 0).reshape(
            block_len, head_count, HD
        )
        value_block = lax.dynamic_slice_in_dim(value_piece, offset, block_len, 0).reshape(
            block_len, head_count, HD
        )
        key_pos = offset + jnp.arange(block_len, dtype=jnp.int32)

        def update_block(inner):
            running, totals, accum = inner
            scores = (
                jnp.einsum(
                    "shd,khd->hsk", query_heads, key_block, preferred_element_type=jnp.float32
                )
                * scale
            )
            causal = key_pos[None, None, :] <= positions[None, :, None]
            newtop = jnp.maximum(running, jnp.max(jnp.where(causal, scores, -1e30), axis=2))
            weights = jnp.where(causal, jnp.exp(scores - newtop[:, :, None]), 0.0)
            factor = jnp.exp(running - newtop)
            totals = totals * factor + jnp.sum(weights, axis=2)
            accum = accum * factor.T[:, :, None] + jnp.einsum(
                "hsk,khd->shd",
                weights.astype(jnp.bfloat16),
                value_block,
                preferred_element_type=jnp.float32,
            )
            return (newtop, totals, accum)

        return lax.cond(offset > query_last, lambda inner: inner, update_block, state)

    running, totals, accum = lax.fori_loop(0, piece_len // block_len, step_block, start_state)
    return (accum / totals.T[:, :, None]).reshape(tok_rows, chan_count).astype(jnp.bfloat16)


def local(streams, filters, gain):
    features = filter_all(streams, filters)
    tok_rows = streams.shape[1]
    my_index = lax.axis_index("ctx")
    queries = features[0]
    positions = my_index * tok_rows + jnp.arange(tok_rows, dtype=jnp.int32)
    attended = attend(queries, positions, features[1], features[2])
    wide = attended.astype(jnp.float32)
    power = lax.psum(jnp.sum(wide * wide, axis=1), "grp") / CH
    return (wide * gain[None, :] * lax.rsqrt(power + 1e-06)[:, None]).astype(jnp.bfloat16)


def solution(mesh):
    placed = (P(None, "ctx", "grp"), P(None, "grp", None), P("grp"))
    return jax.shard_map(
        local, mesh=mesh, in_specs=placed, out_specs=P("ctx", "grp"), check_vma=False
    )
```

profile of v0, /device:TPU:24, one launch (start us, length us, event | category | flops | bytes accessed | tf_op | source)
XLA Modules:
  0.0 568.2 jit_solution(7154377040794997620)
XLA Ops:
  6.5 1.2 slice.21
  7.7 3.4 collective-permute-start
  13.0 112.9 %gather_fusion.1 = bf16[16384,3,64]{2,1,0:T(4,128)(2,1)} fusion(bf16[3,64,128]{1,0,2:T(4,128)(2,1)S(1)} %copy.17, s32[16384]{0:T(1024)S(1)} %broadcast_clamp_fusion), kind=kCustom, calls=%fused_computation.1 | custom fusion | bytes 12648448 | tf_op jit(solution)/shard_map/gather | solution.py:33
  125.9 17.2 %copy.21 = bf16[128,128,3,64]{1,0,3,2:T(8,128)(2,1)} copy(bf16[128,128,3,64]{3,2,1,0:T(4,128)(2,1)} %bitcast.81) | data formatting | bytes 12582912 | tf_op jit(solution)/shard_map/gather | solution.py:33
  143.1 112.7 %gather_fusion = bf16[16384,3,64]{2,1,0:T(4,128)(2,1)} fusion(bf16[3,64,128]{1,0,2:T(4,128)(2,1)S(1)} %copy.17, s32[16384]{0:T(1024)S(1)} %broadcast_clamp_fusion.1), kind=kCustom, calls=%fused_computation | custom fusion | bytes 12648448 | tf_op jit(solution)/shard_map/gather | solution.py:32
  255.9 17.2 %copy.18 = bf16[128,128,3,64]{1,0,3,2:T(8,128)(2,1)} copy(bf16[128,128,3,64]{3,2,1,0:T(4,128)(2,1)} %bitcast.80) | data formatting | bytes 12582912 | tf_op jit(solution)/shard_map/gather | solution.py:32
  273.1 2.1 pad_maximum_fusion
  275.2 3.0 copy.15
  278.2 5.7 %reshape.74 = bf16[3,4,128,64,16]{2,1,4,3,0:T(4,128)(2,1)} reshape(bf16[3,512,1024]{1,2,0:T(8,128)(2,1)} %copy.15) | data formatting | bytes 6291456 | tf_op jit(solution)/shard_map/reshape | solution.py:28
  283.9 8.0 %fusion.40 = (bf16[3,3,128,64,16]{2,1,4,3,0:T(4,128)(2,1)}, bf16[3,3,128,64,16]{2,1,4,3,0:T(4,128)(2,1)S(1)}) fusion(bf16[3,4,128,64,16]{2,1,4,3,0:T(4,128)(2,1)} %reshape.74), kind=kLoop, calls=%fused_computation.56 | loop fusion | bytes 9437184 | tf_op jit(solution)/shard_map/slice | solution.py:35
  292.0 6.0 %fusion.18 = f32[3,64,3,16,128]{4,3,2,1,0:T(8,128)} fusion(bf16[128,128,3,64]{1,0,3,2:T(8,128)(2,1)S(1)} %bitcast.79, pred[128,128]{1,0:T(8,128)(4,1)S(1)} %bitcast.89, bf16[3,3,128,64,16]{2,1,4,3,0:T(4,128)(2,1)S(1)} %get-tuple-element.351), kind=kOutput, calls=%fused_computation.26 | convolution fusion | flops 305135616 | bytes 13385728 | tf_op jit(solution)/shard_map/agts,absgc->abtgc/dot_general | solution.py:37
  298.1 7.8 %fusion.28 = bf16[3,3,128,64,16]{2,4,1,3,0:T(8,128)(2,1)S(1)} fusion(f32[3,64,3,16,128]{4,3,2,1,0:T(8,128)} %fusion.18, bf16[128,128,3,64]{1,0,3,2:T(8,128)(2,1)S(1)} %bitcast.77, pred[128,128]{1,0:T(8,128)(4,1)S(1)} %bitcast.88, bf16[3,3,128,64,16]{2,1,4,3,0:T(4,128)(2,1)} %get-tuple-element.350), kind=kOutput, calls=%fused_computation.38 | convolution fusion | flops 307494912 | bytes 15745024 | tf_op jit(solution)/shard_map/agts,absgc->abtgc/dot_general | solution.py:34
  308.6 1.1 copy.46
  312.0 93.6 %all-gather.3.cloned.1.call-done = bf16[3072,1024]{0,1:T(8,128)(2,1)} async-done(((bf16[384,1024]{0,1:T(8,128)(2,1)}), bf16[3072,1024]{0,1:T(8,128)(2,1)}) %all-gather.3.cloned.1.call-update) | async-done | bytes 6291472 | tf_op jit(solution)/shard_map/all_gather | solution.py:54
  405.6 99.8 %all-gather.5.cloned.1.call-done = bf16[3072,1024]{0,1:T(8,128)(2,1)} async-done(((bf16[384,1024]{0,1:T(8,128)(2,1)}), bf16[3072,1024]{0,1:T(8,128)(2,1)}) %all-gather.5.cloned.1.call-update) | async-done | bytes 6291472 | tf_op jit(solution)/shard_map/all_gather | solution.py:55
  505.5 47.3 %while.18 = (s32[]{:T(128)}, f32[8,384]{1,0:T(8,128)S(1)}, f32[8,384]{1,0:T(8,128)S(1)}, f32[384,8,128]{2,0,1:T(8,128)S(1)}, s32[]{:T(128)}, /*index=5*/bf16[307...) while((s32[]{:T(128)}, f32[8,384]{1,0:T(8,128)S(1)}, ...), condition=%wide.region_6.7_spmd.clone, body=%wide.region_1.6_spmd.clone.sunk | while | flops 823601024 | bytes 30095668 | solution.py:92
  506.2 7.3 %conditional.3 = (f32[8,384]{1,0:T(8,128)S(1)}, f32[8,384]{1,0:T(8,128)S(1)}, f32[384,8,128]{2,0,1:T(8,128)S(1)}) conditional(s32[]{:T(128)} %convert_element_type.65, (s32[]{:T(128)}, s32[512]{0:T(512)S(1)}, s32[]{:T(128)}, bf16[3072,1024]{0,1:T(8,128)(2,1)}, bf16[384,8,128]{2,0,1:T(8,128)(2,1)S(1)}, /*index=5*/f32[8,384]{1,0:T(8,128)S(1)}, ...), branch_computations={%region_2.4_spmd, %region_5.5_spmd} | conditional | flops 823601024 | bytes 30067270 | solution.py:90
  506.2 1.7 constant_dynamic-slice_fusion
  508.1 1.5 fusion.2
  509.6 2.5 bitcast_add_fusion
  512.1 1.3 fusion.6
  514.0 7.3 %conditional.3 = (f32[8,384]{1,0:T(8,128)S(1)}, f32[8,384]{1,0:T(8,128)S(1)}, f32[384,8,128]{2,0,1:T(8,128)S(1)}) conditional(s32[]{:T(128)} %convert_element_type.65, (s32[]{:T(128)}, s32[512]{0:T(512)S(1)}, s32[]{:T(128)}, bf16[3072,1024]{0,1:T(8,128)(2,1)}, bf16[384,8,128]{2,0,1:T(8,128)(2,1)S(1)}, /*index=5*/f32[8,384]{1,0:T(8,128)S(1)}, ...), branch_computations={%region_2.4_spmd, %region_5.5_spmd} | conditional | flops 823601024 | bytes 30067270 | solution.py:90
  514.1 1.7 constant_dynamic-slice_fusion
  516.0 1.5 fusion.2
  517.5 2.5 bitcast_add_fusion
  520.0 1.3 fusion.6
  521.9 7.3 %conditional.3 = (f32[8,384]{1,0:T(8,128)S(1)}, f32[8,384]{1,0:T(8,128)S(1)}, f32[384,8,128]{2,0,1:T(8,128)S(1)}) conditional(s32[]{:T(128)} %convert_element_type.65, (s32[]{:T(128)}, s32[512]{0:T(512)S(1)}, s32[]{:T(128)}, bf16[3072,1024]{0,1:T(8,128)(2,1)}, bf16[384,8,128]{2,0,1:T(8,128)(2,1)S(1)}, /*index=5*/f32[8,384]{1,0:T(8,128)S(1)}, ...), branch_computations={%region_2.4_spmd, %region_5.5_spmd} | conditional | flops 823601024 | bytes 30067270 | solution.py:90
  521.9 1.7 constant_dynamic-slice_fusion
  523.8 1.5 fusion.2
  525.4 2.5 bitcast_add_fusion
  527.8 1.3 fusion.6
  529.8 7.3 %conditional.3 = (f32[8,384]{1,0:T(8,128)S(1)}, f32[8,384]{1,0:T(8,128)S(1)}, f32[384,8,128]{2,0,1:T(8,128)S(1)}) conditional(s32[]{:T(128)} %convert_element_type.65, (s32[]{:T(128)}, s32[512]{0:T(512)S(1)}, s32[]{:T(128)}, bf16[3072,1024]{0,1:T(8,128)(2,1)}, bf16[384,8,128]{2,0,1:T(8,128)(2,1)S(1)}, /*index=5*/f32[8,384]{1,0:T(8,128)S(1)}, ...), branch_computations={%region_2.4_spmd, %region_5.5_spmd} | conditional | flops 823601024 | bytes 30067270 | solution.py:90
  529.8 1.7 constant_dynamic-slice_fusion
  531.7 1.5 fusion.2
  533.2 2.5 bitcast_add_fusion
  535.7 1.3 fusion.6
  537.7 7.3 %conditional.3 = (f32[8,384]{1,0:T(8,128)S(1)}, f32[8,384]{1,0:T(8,128)S(1)}, f32[384,8,128]{2,0,1:T(8,128)S(1)}) conditional(s32[]{:T(128)} %convert_element_type.65, (s32[]{:T(128)}, s32[512]{0:T(512)S(1)}, s32[]{:T(128)}, bf16[3072,1024]{0,1:T(8,128)(2,1)}, bf16[384,8,128]{2,0,1:T(8,128)(2,1)S(1)}, /*index=5*/f32[8,384]{1,0:T(8,128)S(1)}, ...), branch_computations={%region_2.4_spmd, %region_5.5_spmd} | conditional | flops 823601024 | bytes 30067270 | solution.py:90
  537.7 1.7 constant_dynamic-slice_fusion
  539.6 1.5 fusion.2
  541.1 2.5 bitcast_add_fusion
  543.6 1.3 fusion.6
  545.6 7.3 %conditional.3 = (f32[8,384]{1,0:T(8,128)S(1)}, f32[8,384]{1,0:T(8,128)S(1)}, f32[384,8,128]{2,0,1:T(8,128)S(1)}) conditional(s32[]{:T(128)} %convert_element_type.65, (s32[]{:T(128)}, s32[512]{0:T(512)S(1)}, s32[]{:T(128)}, bf16[3072,1024]{0,1:T(8,128)(2,1)}, bf16[384,8,128]{2,0,1:T(8,128)(2,1)S(1)}, /*index=5*/f32[8,384]{1,0:T(8,128)S(1)}, ...), branch_computations={%region_2.4_spmd, %region_5.5_spmd} | conditional | flops 823601024 | bytes 30067270 | solution.py:90
  545.6 1.7 constant_dynamic-slice_fusion
  547.5 1.5 fusion.2
  549.0 2.5 bitcast_add_fusion
  551.5 1.3 fusion.6
  553.4 6.8 %psum.7 = f32[384]{0:T(512)S(1)} all-reduce(f32[384]{0:T(512)S(1)} %get-tuple-element.344), channel_id=1, replica_groups=mesh['ctx'=8,'grp'=4] {'grp'}, use_global_device_ids=true, to_apply=%region_8.9 | all-reduce | flops 384 | bytes 3072 | tf_op jit(solution)/shard_map/psum | solution.py:104
  560.3 1.1 fusion.37
  (87 shorter events, 8.8 us)
Async XLA Ops:
  6.5 399.1 %all-gather.3.cloned.1.call-start = ((), (), s32[]{:S(2)}) async-start(), calls=%async_computation | async-start | bytes 7077888 | tf_op jit(solution)/shard_map/all_gather | solution.py:54
  7.7 265.4 %collective-permute-start = (bf16[3,128,1024]{2,1,0:T(8,128)(2,1)S(1)}, bf16[3,128,1024]{2,1,0:T(8,128)(2,1)}, u32[]{:S(2)}, u32[]{:S(2)}) collective-permute-start(bf16[3,128,1024]{2,1,0:T(8,128)(2,1)S(1)} %slice.21), channel_id=1, source_target_pairs={{0,4},{4,8},{8,12},{12,16},{16,20},{20,24},{24,28},{1,5},{5,9},{9,... | collective-permute-start | bytes 2359304 | tf_op jit(solution)/shard_map/ppermute | solution.py:15
  125.9 17.3 %copy-start.2 = (s32[16384]{0:T(1024)S(1)}, s32[16384]{0:T(1024)}, u32[]{:S(2)}) copy-start(s32[16384]{0:T(1024)} %constant.103) | copy-start | bytes 196612
  278.2 13.7 %slice-start.2 = ((s8[6291456]{0:T(1024)(128)(4,1)}), s8[2097152]{0:T(1024)(128)(4,1)S(1)}, s32[]{:S(2)}) async-start(s8[6291456]{0:T(1024)(128)(4,1)} %bitcast.78), calls=%async_computation.4 | async-start | bytes 4194304
  283.9 8.1 %slice-start.3 = ((s8[6291456]{0:T(1024)(128)(4,1)}), s8[4194304]{0:T(1024)(128)(4,1)S(1)}, s32[]{:S(2)}) async-start(s8[6291456]{0:T(1024)(128)(4,1)} %bitcast.78), calls=%async_computation.5 | async-start | bytes 8388608
  283.9 8.1 %copy-start.1 = (pred[128,128]{1,0:T(32,128)(4,1)S(1)}, pred[128,128]{1,0:T(32,128)(4,1)}, u32[]{:S(2)}) copy-start(pred[128,128]{1,0:T(32,128)(4,1)} %constant.100.clone) | copy-start | bytes 49156
  283.9 14.1 %slice-start = ((s8[6291456]{0:T(1024)(128)(4,1)}), s8[4194304]{0:T(1024)(128)(4,1)S(1)}, s32[]{:S(2)}) async-start(s8[6291456]{0:T(1024)(128)(4,1)} %bitcast.76), calls=%async_computation.2 | async-start | bytes 8388608
  292.0 6.1 %slice-start.1 = ((s8[6291456]{0:T(1024)(128)(4,1)}), s8[2097152]{0:T(1024)(128)(4,1)S(1)}, s32[]{:S(2)}) async-start(s8[6291456]{0:T(1024)(128)(4,1)} %bitcast.76), calls=%async_computation.3 | async-start | bytes 4194304
  292.0 6.1 %copy-start = (pred[128,128]{1,0:T(32,128)(4,1)S(1)}, pred[128,128]{1,0:T(32,128)(4,1)}, u32[]{:S(2)}) copy-start(pred[128,128]{1,0:T(32,128)(4,1)} %constant.98.clone) | copy-start | bytes 49156
  307.9 197.5 %all-gather.5.cloned.1.call-start = ((), (), s32[]{:S(2)}) async-start(), calls=%async_computation.1 | async-start | bytes 7077888 | tf_op jit(solution)/shard_map/all_gather | solution.py:55
  505.5 54.7 %copy-start.3 = (f32[1024]{0:T(1024)S(1)}, f32[1024]{0:T(1024)}, u32[]{:S(2)}) copy-start(f32[1024]{0:T(1024)} %param.15) | copy-start | bytes 12292
Sparse Core Ops, SparseCore 0:
  308.0 97.6 all-gather.2
  407.7 97.6 all-gather.4
where the time goes:
time: 570 us; the launch traced here: 568 us
  local copies, waits for them, and re-layouts  294 us (52%)
  waiting for transfers between devices  193 us (34%)
  matrix products  37.7 us (7%)
  other arithmetic  14.4 us (3%)
  between operations  13.6 us (2%)
  blocking collectives  6.84 us (1%)
    gather x2, local copies, waits for them, and re-layouts, filter_all(): upper = jnp.where(lag_table < 0, filters[:, :, upper_idx], 0.0)  130 us
    gather x2, local copies, waits for them, and re-layouts, filter_all(): lower = jnp.where(lag_table >= 0, filters[:, :, lower_idx], 0.0)  130 us
    all_gather x1, waiting for transfers between devices, attend(): value_piece = lax.all_gather(valued, 'ctx', axis=0, tiled=True)  99.8 us
    all_gather x1, waiting for transfers between devices, attend(): key_piece = lax.all_gather(keyed, 'ctx', axis=0, tiled=True)  93.6 us
    dot_general x6, matrix products, update_block(): jnp.einsum('hsk,khd->shd', weights.astype(jnp.bfloat16), value_block, pre...  14.9 us
  transfers between devices with their start and end apart: 3, of which 2 were waited for; matrix products, arithmetic and copies ran while one was open for 47% of the time, Pallas kernels for 0%

commit v1 on v0

--- a/solution.py
+++ b/solution.py
@@ -7,6 +7,22 @@
 
 HD = 128
 CH = 4096
+
+
+def report_tasks(row_axis, xin):
+    k_all = lax.psum(1, row_axis)
+    val2 = range(k_all)
+    newest = map(lambda jj: (jj, (jj + 1) % k_all), val2)
+    last = [None] * k_all
+    last[k_all - 1] = xin
+    by_rank = list(newest)
+    for d in range(k_all - 2, -1, -1):
+        last[d] = lax.ppermute(last[d + 1], row_axis, by_rank)
+    a_now = jnp.concatenate(last, 0)
+    arr_now = lax.axis_index(row_axis)
+    long_array = (arr_now + 1) * xin.shape[0]
+    top = jnp.roll(a_now, long_array, 0)
+    return top
 
 
 def passed_along(block, axis, distance):
@@ -52,7 +68,7 @@
         jnp.zeros((tok_rows, head_count, HD), jnp.float32),
     )
     key_piece = lax.all_gather(keyed, "ctx", axis=0, tiled=True)
-    value_piece = lax.all_gather(valued, "ctx", axis=0, tiled=True)
+    value_piece = report_tasks("ctx", valued)
     piece_len = key_piece.shape[0]
     block_len = math.gcd(piece_len, 512)
 

time: 570 us -> 601 us (1.054)
  local copies, waits for them, and re-layouts: 294 us -> 317 us
  waiting for transfers between devices: 193 us -> 203 us
    ppermute x0 -> x7, waiting for transfers between devices: none -> 203 us  [report_tasks(): last[d] = lax.ppermute(last[d + 1], row_axis, by_rank)]
    all_gather x1 -> x0, waiting for transfers between devices: 99.8 us -> none  [attend(): value_piece = lax.all_gather(valued, 'ctx', axis=0, tiled=True)]
    all_gather x1, waiting for transfers between devices: 93.6 us -> 0.01 us  [attend(): key_piece = lax.all_gather(keyed, 'ctx', axis=0, tiled=True)]
    unnamed x20 -> x55, local copies, waits for them, and re-layouts: 3.46 us -> 19.6 us
    dynamic_slice x0 -> x1, local copies, waits for them, and re-layouts: none -> 6.15 us  [report_tasks(): top = jnp.roll(a_now, long_array, 0)]
  transfers between devices with their start and end apart: 3 -> 9, of which waited for: 2 -> 7; matrix products, arithmetic and copies ran while one was open for 47% -> 47% of each run, Pallas kernels for 0% -> 0%
where the time goes in v1:
time: 601 us; the launch traced here: 599 us
  local copies, waits for them, and re-layouts  317 us (53%)
  waiting for transfers between devices  203 us (34%)
  matrix products  37.7 us (6%)
  other arithmetic  14.4 us (2%)
  between operations  13.8 us (2%)
    ppermute x7, waiting for transfers between devices, report_tasks(): last[d] = lax.ppermute(last[d + 1], row_axis, by_rank)  203 us
    gather x2, local copies, waits for them, and re-layouts, filter_all(): upper = jnp.where(lag_table < 0, filters[:, :, upper_idx], 0.0)  130 us
    gather x2, local copies, waits for them, and re-layouts, filter_all(): lower = jnp.where(lag_table >= 0, filters[:, :, lower_idx], 0.0)  130 us
    unnamed x55, local copies, waits for them, and re-layouts  19.6 us
    dot_general x6, matrix products, update_block(): jnp.einsum('hsk,khd->shd', weights.astype(jnp.bfloat16), value_block, pre...  14.9 us
  transfers between devices with their start and end apart: 9, of which 7 were waited for; matrix products, arithmetic and copies ran while one was open for 47% of the time, Pallas kernels for 0%

profile of v1, /device:TPU:24, one launch (start us, length us, event | category | flops | bytes accessed | tf_op | source)
XLA Modules:
  0.0 599.4 jit_solution(17689433364415602130)
XLA Ops:
  7.7 3.4 collective-permute-start
  13.0 112.7 %gather_fusion.1 = bf16[16384,3,64]{2,1,0:T(4,128)(2,1)} fusion(bf16[3,64,128]{1,0,2:T(4,128)(2,1)S(1)} %copy.17, s32[16384]{0:T(1024)S(1)} %broadcast_clamp_fusion), kind=kCustom, calls=%fused_computation.1 | custom fusion | bytes 12648448 | tf_op jit(solution)/shard_map/gather | solution.py:49
  125.7 17.2 %copy.21 = bf16[128,128,3,64]{1,0,3,2:T(8,128)(2,1)} copy(bf16[128,128,3,64]{3,2,1,0:T(4,128)(2,1)} %bitcast.85) | data formatting | bytes 12582912 | tf_op jit(solution)/shard_map/gather | solution.py:49
  143.0 112.6 %gather_fusion = bf16[16384,3,64]{2,1,0:T(4,128)(2,1)} fusion(bf16[3,64,128]{1,0,2:T(4,128)(2,1)S(1)} %copy.17, s32[16384]{0:T(1024)S(1)} %broadcast_clamp_fusion.1), kind=kCustom, calls=%fused_computation | custom fusion | bytes 12648448 | tf_op jit(solution)/shard_map/gather | solution.py:48
  255.5 17.2 %copy.18 = bf16[128,128,3,64]{1,0,3,2:T(8,128)(2,1)} copy(bf16[128,128,3,64]{3,2,1,0:T(4,128)(2,1)} %bitcast.84) | data formatting | bytes 12582912 | tf_op jit(solution)/shard_map/gather | solution.py:48
  272.7 2.1 pad_maximum_fusion
  274.9 3.0 copy.15
  277.8 5.6 reshape.74
  283.5 8.1 %fusion.40 = (bf16[3,3,128,64,16]{2,1,4,3,0:T(4,128)(2,1)}, bf16[3,3,128,64,16]{2,1,4,3,0:T(4,128)(2,1)S(1)}) fusion(bf16[3,4,128,64,16]{2,1,4,3,0:T(4,128)(2,1)} %reshape.74), kind=kLoop, calls=%fused_computation.73 | loop fusion | bytes 9437184 | tf_op jit(solution)/shard_map/slice | solution.py:51
  291.6 6.0 %fusion.18 = f32[3,64,3,16,128]{4,3,2,1,0:T(8,128)} fusion(bf16[128,128,3,64]{1,0,3,2:T(8,128)(2,1)S(1)} %bitcast.83, pred[128,128]{1,0:T(8,128)(4,1)S(1)} %bitcast.95, bf16[3,3,128,64,16]{2,1,4,3,0:T(4,128)(2,1)S(1)} %get-tuple-element.351), kind=kOutput, calls=%fused_computation.26 | convolution fusion | flops 305135616 | bytes 13385728 | tf_op jit(solution)/shard_map/agts,absgc->abtgc/dot_general | solution.py:53
  297.7 7.8 %fusion.28 = bf16[3,3,128,64,16]{2,4,1,3,0:T(8,128)(2,1)S(1)} fusion(f32[3,64,3,16,128]{4,3,2,1,0:T(8,128)} %fusion.18, bf16[128,128,3,64]{1,0,3,2:T(8,128)(2,1)S(1)} %bitcast.81, pred[128,128]{1,0:T(8,128)(4,1)S(1)} %bitcast.94, bf16[3,3,128,64,16]{2,1,4,3,0:T(4,128)(2,1)} %get-tuple-element.350), kind=kOutput, calls=%fused_computation.38 | convolution fusion | flops 307494912 | bytes 15745024 | tf_op jit(solution)/shard_map/agts,absgc->abtgc/dot_general | solution.py:50
  308.2 28.3 %collective-permute-done.1 = bf16[384,1024]{0,1:T(8,128)(2,1)S(1)} collective-permute-done((bf16[384,1024]{0,1:T(8,128)(2,1)S(1)}, bf16[384,1024]{0,1:T(8,128)(2,1)S(1)}, u32[]{:S(2)}, u32[]{:S(2)}) %collective-permute-start.1) | collective-permute-done | bytes 786464 | tf_op jit(solution)/shard_map/ppermute | solution.py:20
  337.5 33.2 %collective-permute-done.2 = bf16[384,1024]{0,1:T(8,128)(2,1)S(1)} collective-permute-done((bf16[384,1024]{0,1:T(8,128)(2,1)S(1)}, bf16[384,1024]{0,1:T(8,128)(2,1)S(1)}, u32[]{:S(2)}, u32[]{:S(2)}) %collective-permute-start.2) | collective-permute-done | bytes 786464 | tf_op jit(solution)/shard_map/ppermute | solution.py:20
  371.6 46.8 %collective-permute-done.3 = bf16[384,1024]{0,1:T(8,128)(2,1)S(1)} collective-permute-done((bf16[384,1024]{0,1:T(8,128)(2,1)S(1)}, bf16[384,1024]{0,1:T(8,128)(2,1)S(1)}, u32[]{:S(2)}, u32[]{:S(2)}) %collective-permute-start.3) | collective-permute-done | bytes 786464 | tf_op jit(solution)/shard_map/ppermute | solution.py:20
  419.3 41.5 %collective-permute-done.4 = bf16[384,1024]{0,1:T(8,128)(2,1)S(1)} collective-permute-done((bf16[384,1024]{0,1:T(8,128)(2,1)S(1)}, bf16[384,1024]{0,1:T(8,128)(2,1)S(1)}, u32[]{:S(2)}, u32[]{:S(2)}) %collective-permute-start.4) | collective-permute-done | bytes 786464 | tf_op jit(solution)/shard_map/ppermute | solution.py:20
  461.6 19.7 %collective-permute-done.5 = bf16[384,1024]{0,1:T(8,128)(2,1)S(1)} collective-permute-done((bf16[384,1024]{0,1:T(8,128)(2,1)S(1)}, bf16[384,1024]{0,1:T(8,128)(2,1)S(1)}, u32[]{:S(2)}, u32[]{:S(2)}) %collective-permute-start.5) | collective-permute-done | bytes 786464 | tf_op jit(solution)/shard_map/ppermute | solution.py:20
  482.3 19.0 %collective-permute-done.6 = bf16[384,1024]{0,1:T(8,128)(2,1)} collective-permute-done((bf16[384,1024]{0,1:T(8,128)(2,1)S(1)}, bf16[384,1024]{0,1:T(8,128)(2,1)}, u32[]{:S(2)}, u32[]{:S(2)}) %collective-permute-start.6) | collective-permute-done | bytes 786464 | tf_op jit(solution)/shard_map/ppermute | solution.py:20
  502.4 1.4 reshape_squeeze.3
  503.9 1.6 copy.25
  505.5 14.1 %collective-permute-done.7 = bf16[384,1024]{0,1:T(8,128)(2,1)} collective-permute-done((bf16[384,1024]{0,1:T(8,128)(2,1)}, bf16[384,1024]{0,1:T(8,128)(2,1)}, u32[]{:S(2)}, u32[]{:S(2)}) %collective-permute-start.7) | collective-permute-done | bytes 786464 | tf_op jit(solution)/shard_map/ppermute | solution.py:20
  523.7 1.4 constant_dynamic-update-slice_fusion.12
  531.4 6.2 %constant_dynamic-slice_fusion.2 = bf16[3072,1024]{0,1:T(8,128)(2,1)} fusion(bf16[6144,1024]{0,1:T(8,128)(2,1)S(1)} %constant_dynamic-update-slice_fusion, s32[]{:T(128)S(6)} %select_n.54), kind=kLoop, calls=%fused_computation.70 | loop fusion | bytes 12582916 | tf_op jit(solution)/shard_map/jit(_roll_dynamic)/dynamic_slice | solution.py:24
  537.7 47.5 %while.18 = (s32[]{:T(128)}, f32[8,384]{1,0:T(8,128)S(1)}, f32[8,384]{1,0:T(8,128)S(1)}, f32[384,8,128]{2,0,1:T(8,128)S(1)}, s32[]{:T(128)}, /*index=5*/bf16[307...) while((s32[]{:T(128)}, f32[8,384]{1,0:T(8,128)S(1)}, ...), condition=%wide.region_6.7_spmd.clone, body=%wide.region_1.6_spmd.clone.sunk | while | flops 823601024 | bytes 30095668 | solution.py:108
  538.5 7.3 %conditional.3 = (f32[8,384]{1,0:T(8,128)S(1)}, f32[8,384]{1,0:T(8,128)S(1)}, f32[384,8,128]{2,0,1:T(8,128)S(1)}) conditional(s32[]{:T(128)} %convert_element_type.65, (s32[]{:T(128)}, s32[512]{0:T(512)S(1)}, s32[]{:T(128)}, bf16[3072,1024]{0,1:T(8,128)(2,1)}, bf16[384,8,128]{2,0,1:T(8,128)(2,1)S(1)}, /*index=5*/f32[8,384]{1,0:T(8,128)S(1)}, ...), branch_computations={%region_2.4_spmd, %region_5.5_spmd} | conditional | flops 823601024 | bytes 30067270 | solution.py:106
  538.5 1.7 constant_dynamic-slice_fusion
  540.4 1.5 fusion.2
  542.0 2.5 bitcast_add_fusion
  546.4 7.3 %conditional.3 = (f32[8,384]{1,0:T(8,128)S(1)}, f32[8,384]{1,0:T(8,128)S(1)}, f32[384,8,128]{2,0,1:T(8,128)S(1)}) conditional(s32[]{:T(128)} %convert_element_type.65, (s32[]{:T(128)}, s32[512]{0:T(512)S(1)}, s32[]{:T(128)}, bf16[3072,1024]{0,1:T(8,128)(2,1)}, bf16[384,8,128]{2,0,1:T(8,128)(2,1)S(1)}, /*index=5*/f32[8,384]{1,0:T(8,128)S(1)}, ...), branch_computations={%region_2.4_spmd, %region_5.5_spmd} | conditional | flops 823601024 | bytes 30067270 | solution.py:106
  546.4 1.7 constant_dynamic-slice_fusion
  548.3 1.5 fusion.2
  549.8 2.5 bitcast_add_fusion
  554.3 7.3 %conditional.3 = (f32[8,384]{1,0:T(8,128)S(1)}, f32[8,384]{1,0:T(8,128)S(1)}, f32[384,8,128]{2,0,1:T(8,128)S(1)}) conditional(s32[]{:T(128)} %convert_element_type.65, (s32[]{:T(128)}, s32[512]{0:T(512)S(1)}, s32[]{:T(128)}, bf16[3072,1024]{0,1:T(8,128)(2,1)}, bf16[384,8,128]{2,0,1:T(8,128)(2,1)S(1)}, /*index=5*/f32[8,384]{1,0:T(8,128)S(1)}, ...), branch_computations={%region_2.4_spmd, %region_5.5_spmd} | conditional | flops 823601024 | bytes 30067270 | solution.py:106
  554.3 1.7 constant_dynamic-slice_fusion
  556.2 1.5 fusion.2
  557.7 2.5 bitcast_add_fusion
  562.2 7.3 %conditional.3 = (f32[8,384]{1,0:T(8,128)S(1)}, f32[8,384]{1,0:T(8,128)S(1)}, f32[384,8,128]{2,0,1:T(8,128)S(1)}) conditional(s32[]{:T(128)} %convert_element_type.65, (s32[]{:T(128)}, s32[512]{0:T(512)S(1)}, s32[]{:T(128)}, bf16[3072,1024]{0,1:T(8,128)(2,1)}, bf16[384,8,128]{2,0,1:T(8,128)(2,1)S(1)}, /*index=5*/f32[8,384]{1,0:T(8,128)S(1)}, ...), branch_computations={%region_2.4_spmd, %region_5.5_spmd} | conditional | flops 823601024 | bytes 30067270 | solution.py:106
  562.2 1.7 constant_dynamic-slice_fusion
  564.1 1.5 fusion.2
  565.6 2.5 bitcast_add_fusion
  570.0 7.3 %conditional.3 = (f32[8,384]{1,0:T(8,128)S(1)}, f32[8,384]{1,0:T(8,128)S(1)}, f32[384,8,128]{2,0,1:T(8,128)S(1)}) conditional(s32[]{:T(128)} %convert_element_type.65, (s32[]{:T(128)}, s32[512]{0:T(512)S(1)}, s32[]{:T(128)}, bf16[3072,1024]{0,1:T(8,128)(2,1)}, bf16[384,8,128]{2,0,1:T(8,128)(2,1)S(1)}, /*index=5*/f32[8,384]{1,0:T(8,128)S(1)}, ...), branch_computations={%region_2.4_spmd, %region_5.5_spmd} | conditional | flops 823601024 | bytes 30067270 | solution.py:106
  570.1 1.7 constant_dynamic-slice_fusion
  571.9 1.5 fusion.2
  573.5 2.5 bitcast_add_fusion
  577.9 7.3 %conditional.3 = (f32[8,384]{1,0:T(8,128)S(1)}, f32[8,384]{1,0:T(8,128)S(1)}, f32[384,8,128]{2,0,1:T(8,128)S(1)}) conditional(s32[]{:T(128)} %convert_element_type.65, (s32[]{:T(128)}, s32[512]{0:T(512)S(1)}, s32[]{:T(128)}, bf16[3072,1024]{0,1:T(8,128)(2,1)}, bf16[384,8,128]{2,0,1:T(8,128)(2,1)S(1)}, /*index=5*/f32[8,384]{1,0:T(8,128)S(1)}, ...), branch_computations={%region_2.4_spmd, %region_5.5_spmd} | conditional | flops 823601024 | bytes 30067270 | solution.py:106
  577.9 1.7 constant_dynamic-slice_fusion
  579.8 1.5 fusion.2
  581.3 2.5 bitcast_add_fusion
  585.8 5.7 psum.7
  (135 shorter events, 32.5 us)
Async XLA Ops:
  6.5 531.0 %all-gather.2.cloned.1.call-start = ((), (), s32[]{:S(2)}) async-start(), calls=%async_computation | async-start | bytes 7077888 | tf_op jit(solution)/shard_map/all_gather | solution.py:70
  7.7 265.0 %collective-permute-start = (bf16[3,128,1024]{2,1,0:T(8,128)(2,1)S(1)}, bf16[3,128,1024]{2,1,0:T(8,128)(2,1)}, u32[]{:S(2)}, u32[]{:S(2)}) collective-permute-start(bf16[3,128,1024]{2,1,0:T(8,128)(2,1)S(1)} %slice.21), channel_id=1, source_target_pairs={{0,4},{4,8},{8,12},{12,16},{16,20},{20,24},{24,28},{1,5},{5,9},{9,... | collective-permute-start | bytes 2359304 | tf_op jit(solution)/shard_map/ppermute | solution.py:31
  125.7 17.2 %copy-start.12 = (s32[16384]{0:T(1024)S(1)}, s32[16384]{0:T(1024)}, u32[]{:S(2)}) copy-start(s32[16384]{0:T(1024)} %constant.123) | copy-start | bytes 196612
  277.8 13.7 %slice-start.2 = ((s8[6291456]{0:T(1024)(128)(4,1)}), s8[2097152]{0:T(1024)(128)(4,1)S(1)}, s32[]{:S(2)}) async-start(s8[6291456]{0:T(1024)(128)(4,1)} %bitcast.82), calls=%async_computation.3 | async-start | bytes 4194304
  283.5 8.1 %slice-start.3 = ((s8[6291456]{0:T(1024)(128)(4,1)}), s8[4194304]{0:T(1024)(128)(4,1)S(1)}, s32[]{:S(2)}) async-start(s8[6291456]{0:T(1024)(128)(4,1)} %bitcast.82), calls=%async_computation.4 | async-start | bytes 8388608
  283.5 8.1 %copy-start.11 = (pred[128,128]{1,0:T(32,128)(4,1)S(1)}, pred[128,128]{1,0:T(32,128)(4,1)}, u32[]{:S(2)}) copy-start(pred[128,128]{1,0:T(32,128)(4,1)} %constant.120.clone) | copy-start | bytes 49156
  283.5 14.2 %slice-start = ((s8[6291456]{0:T(1024)(128)(4,1)}), s8[4194304]{0:T(1024)(128)(4,1)S(1)}, s32[]{:S(2)}) async-start(s8[6291456]{0:T(1024)(128)(4,1)} %bitcast.80), calls=%async_computation.1 | async-start | bytes 8388608
  291.6 6.1 %slice-start.1 = ((s8[6291456]{0:T(1024)(128)(4,1)}), s8[2097152]{0:T(1024)(128)(4,1)S(1)}, s32[]{:S(2)}) async-start(s8[6291456]{0:T(1024)(128)(4,1)} %bitcast.80), calls=%async_computation.2 | async-start | bytes 4194304
  291.6 6.1 %copy-start.10 = (pred[128,128]{1,0:T(32,128)(4,1)S(1)}, pred[128,128]{1,0:T(32,128)(4,1)}, u32[]{:S(2)}) copy-start(pred[128,128]{1,0:T(32,128)(4,1)} %constant.118.clone) | copy-start | bytes 49156
  308.2 28.4 %collective-permute-start.1 = (bf16[384,1024]{0,1:T(8,128)(2,1)S(1)}, bf16[384,1024]{0,1:T(8,128)(2,1)S(1)}, u32[]{:S(2)}, u32[]{:S(2)}) collective-permute-start(bf16[384,1024]{0,1:T(8,128)(2,1)S(1)} %bitcast.92), channel_id=1, source_target_pairs={{0,4},{4,8},{8,12},{12,16},{16,20},{20,24},{24,28},{28,0},{1,5},{5... | collective-permute-start | bytes 2359304 | tf_op jit(solution)/shard_map/ppermute | solution.py:20
  336.6 0.9 copy-start
  337.5 33.2 %collective-permute-start.2 = (bf16[384,1024]{0,1:T(8,128)(2,1)S(1)}, bf16[384,1024]{0,1:T(8,128)(2,1)S(1)}, u32[]{:S(2)}, u32[]{:S(2)}) collective-permute-start(bf16[384,1024]{0,1:T(8,128)(2,1)S(1)} %collective-permute-done.1), channel_id=1, source_target_pairs={{0,4},{4,8},{8,12},{12,16},{16,20},{20,24},{24,28},{28,0},{1,5},{5... | collective-permute-start | bytes 2359304 | tf_op jit(solution)/shard_map/ppermute | solution.py:20
  370.7 0.9 copy-start.2
  371.6 46.8 %collective-permute-start.3 = (bf16[384,1024]{0,1:T(8,128)(2,1)S(1)}, bf16[384,1024]{0,1:T(8,128)(2,1)S(1)}, u32[]{:S(2)}, u32[]{:S(2)}) collective-permute-start(bf16[384,1024]{0,1:T(8,128)(2,1)S(1)} %collective-permute-done.2), channel_id=1, source_target_pairs={{0,4},{4,8},{8,12},{12,16},{16,20},{20,24},{24,28},{28,0},{1,5},{5... | collective-permute-start | bytes 2359304 | tf_op jit(solution)/shard_map/ppermute | solution.py:20
  418.4 0.9 copy-start.4
  419.3 41.5 %collective-permute-start.4 = (bf16[384,1024]{0,1:T(8,128)(2,1)S(1)}, bf16[384,1024]{0,1:T(8,128)(2,1)S(1)}, u32[]{:S(2)}, u32[]{:S(2)}) collective-permute-start(bf16[384,1024]{0,1:T(8,128)(2,1)S(1)} %collective-permute-done.3), channel_id=1, source_target_pairs={{0,4},{4,8},{8,12},{12,16},{16,20},{20,24},{24,28},{28,0},{1,5},{5... | collective-permute-start | bytes 2359304 | tf_op jit(solution)/shard_map/ppermute | solution.py:20
  460.7 0.9 copy-start.6
  461.6 19.7 %collective-permute-start.5 = (bf16[384,1024]{0,1:T(8,128)(2,1)S(1)}, bf16[384,1024]{0,1:T(8,128)(2,1)S(1)}, u32[]{:S(2)}, u32[]{:S(2)}) collective-permute-start(bf16[384,1024]{0,1:T(8,128)(2,1)S(1)} %collective-permute-done.4), channel_id=1, source_target_pairs={{0,4},{4,8},{8,12},{12,16},{16,20},{20,24},{24,28},{28,0},{1,5},{5... | collective-permute-start | bytes 2359304 | tf_op jit(solution)/shard_map/ppermute | solution.py:20
  481.4 0.9 copy-start.8
  482.3 19.0 %collective-permute-start.6 = (bf16[384,1024]{0,1:T(8,128)(2,1)S(1)}, bf16[384,1024]{0,1:T(8,128)(2,1)}, u32[]{:S(2)}, u32[]{:S(2)}) collective-permute-start(bf16[384,1024]{0,1:T(8,128)(2,1)S(1)} %collective-permute-done.5), channel_id=1, source_target_pairs={{0,4},{4,8},{8,12},{12,16},{16,20},{20,24},{24,28},{28,0},{1,5},{5... | collective-permute-start | bytes 2359304 | tf_op jit(solution)/shard_map/ppermute | solution.py:20
  501.3 18.3 %collective-permute-start.7 = (bf16[384,1024]{0,1:T(8,128)(2,1)}, bf16[384,1024]{0,1:T(8,128)(2,1)}, u32[]{:S(2)}, u32[]{:S(2)}) collective-permute-start(bf16[384,1024]{0,1:T(8,128)(2,1)} %collective-permute-done.6), channel_id=1, source_target_pairs={{0,4},{4,8},{8,12},{12,16},{16,20},{20,24},{24,28},{28,0},{1,5},{5... | collective-permute-start | bytes 2359304 | tf_op jit(solution)/shard_map/ppermute | solution.py:20
  503.9 21.3 %copy-start.5 = (bf16[384,1024]{0,1:T(8,128)(2,1)S(1)}, bf16[384,1024]{0,1:T(8,128)(2,1)}, u32[]{:S(2)}) copy-start(bf16[384,1024]{0,1:T(8,128)(2,1)} %copy-done.4) | copy-start | bytes 2359300
  503.9 22.9 %copy-start.1 = (bf16[384,1024]{0,1:T(8,128)(2,1)S(1)}, bf16[384,1024]{0,1:T(8,128)(2,1)}, u32[]{:S(2)}) copy-start(bf16[384,1024]{0,1:T(8,128)(2,1)} %copy-done) | copy-start | bytes 2359300
  522.2 7.8 %copy-start.9 = (bf16[384,1024]{0,1:T(8,128)(2,1)S(1)}, bf16[384,1024]{0,1:T(8,128)(2,1)}, u32[]{:S(2)}) copy-start(bf16[384,1024]{0,1:T(8,128)(2,1)} %copy-done.8) | copy-start | bytes 2359300
  523.7 6.5 %copy-start.7 = (bf16[384,1024]{0,1:T(8,128)(2,1)S(1)}, bf16[384,1024]{0,1:T(8,128)(2,1)}, u32[]{:S(2)}) copy-start(bf16[384,1024]{0,1:T(8,128)(2,1)} %copy-done.6) | copy-start | bytes 2359300
  525.4 5.3 copy-start.3
  537.7 53.8 %copy-start.13 = (f32[1024]{0:T(1024)S(1)}, f32[1024]{0:T(1024)}, u32[]{:S(2)}) copy-start(f32[1024]{0:T(1024)} %param.15) | copy-start | bytes 12292
Sparse Core Ops, SparseCore 0:
  307.6 144.3 all-gather.1
